TPU v7x, 32 devices: a whole 2x2x4 slice. The times are simulated.
32 devices in a mesh: row: 4 (over z), col: 2 (over x), depth: 4 (over y, core).
Axes of the slice: x: 2, y: 2, z: 4, core: 2. Of those that a mesh axis runs over, the one named last changes fastest.
Arguments:
- tokens: bfloat16 [2560, 8192], P(('row', 'depth'), 'col'), may hold values from -6 to 6
- weight: bfloat16 [8192, 4096], P('row', 'col'), may hold values from -0.0625 to 0.0625
- cotangent: bfloat16 [2560, 4096], P(('row', 'depth'), 'col'), may hold values from -6 to 6
- master: float32 [8192, 4096], P(('row', 'depth'), 'col'), may hold values from -0.1 to 0.1
- first_moment: float32 [8192, 4096], P(('row', 'depth'), 'col'), may hold values from -6 to 6
- second_moment: float32 [8192, 4096], P(('row', 'depth'), 'col'), may hold values from 0.1 to 10
Outputs:
- queries: bfloat16 [2560, 4096], P(('row', 'depth'), 'col')
- token_grad: bfloat16 [2560, 8192], P(('row', 'depth'), 'col')
- new_master: float32 [8192, 4096], P(('row', 'depth'), 'col')
- new_first: float32 [8192, 4096], P(('row', 'depth'), 'col')
- new_second: float32 [8192, 4096], P(('row', 'depth'), 'col')
- new_weight: bfloat16 [8192, 4096], P('row', 'col')
All inputs are finite; a program needn't handle non-finite values.
Results may differ from a plain program's by a relative error of at most 0.001.
Values may be sent and summed in bfloat16 or wider, within the bound.
A program may use at most 128 MiB of HBM per device.

v0:
```python
import math

import jax
import jax.numpy as jnp
from jax import lax
from jax.sharding import PartitionSpec as P

beta_one = 0.9
beta_two = 0.95
learn_rate = 0.02
decay_rate = 0.1
adam_eps = 1e-08
bias_one = 1.0 - 0.9**50
bias_two = 1.0 - 0.95**50


def local(tokens, weight, cotangent, master, first_moment, second_moment):
    total_tokens = tokens.shape[0] * lax.axis_size("row") * lax.axis_size("depth")
    grad_scale = 1.0 / math.sqrt(total_tokens)
    full_rows = lax.all_gather(tokens, "col", axis=1, tiled=True)
    full_panel = lax.all_gather(weight, "row", axis=0, tiled=True)
    queries = jnp.dot(full_rows, full_panel, preferred_element_type=jnp.float32).astype(
        jnp.bfloat16
    )
    partial_value = lax.dot_general(
        cotangent, full_panel, (((1,), (1,)), ((), ())), preferred_element_type=jnp.float32
    )
    token_grad = lax.psum_scatter(partial_value, "col", scatter_dimension=1, tiled=True).astype(
        jnp.bfloat16
    )
    token_slab = lax.all_to_all(
        full_rows, ("row", "depth"), split_axis=1, concat_axis=0, tiled=True
    )
    product = lax.dot_general(
        token_slab,
        lax.all_gather(cotangent, ("row", "depth"), axis=0, tiled=True),
        (((0,), (0,)), ((), ())),
        preferred_element_type=jnp.float32,
    )
    grad = product * grad_scale
    new_first = beta_one * first_moment + (1.0 - beta_one) * grad
    new_second = beta_two * second_moment + (1.0 - beta_two) * grad * grad
    step_value = new_first / bias_one / (jnp.sqrt(new_second / bias_two) + adam_eps)
    new_master = master - learn_rate * (step_value + decay_rate * master)
    shard_weight = new_master.astype(jnp.bfloat16)
    new_weight = lax.all_gather(shard_weight, "depth", axis=0, tiled=True)
    return (queries, token_grad, new_master, new_first, new_second, new_weight)


def solution(mesh):
    in_specs = (
        P(("row", "depth"), "col"),
        P("row", "col"),
        P(("row", "depth"), "col"),
        P(("row", "depth"), "col"),
        P(("row", "depth"), "col"),
        P(("row", "depth"), "col"),
    )
    out_specs = (
        P(("row", "depth"), "col"),
        P(("row", "depth"), "col"),
        P(("row", "depth"), "col"),
        P(("row", "depth"), "col"),
        P(("row", "depth"), "col"),
        P("row", "col"),
    )
    return jax.shard_map(local, mesh=mesh, in_specs=in_specs, out_specs=out_specs, check_vma=False)
```

profile of v0, /device:TPU:0, one launch (start us, length us, event | category | flops | bytes accessed | tf_op | source)
XLA Modules:
  0.0 889.6 jit_solution(17956850485688772737)
XLA Ops:
  7.2 0.0 all-gather.5.cloned.1.call-start
  7.2 0.7 all-gather.5.cloned.1.call-update
  7.9 0.0 all-gather.9.cloned.1.call-start
  7.9 0.7 all-gather.9.cloned.1.call-update
  8.6 0.0 all-gather.7.cloned.1.call-start
  8.7 0.7 all-gather.7.cloned.1.call-update
  9.4 0.0 all-gather.11.cloned.1.call-start
  9.4 41.8 %all-gather.5.cloned.1.call-done = bf16[160,8192]{1,0:T(8,128)(2,1)} async-done(((bf16[160,4096]{1,0:T(8,128)(2,1)}), bf16[160,8192]{1,0:T(8,128)(2,1)}) %all-gather.5.cloned.1.call-update) | async-done | bytes 2621456 | tf_op jit(solution)/shard_map/all_gather | solution.py:20
  51.3 2.0 copy.16
  53.3 113.0 %all_to_all.19 = bf16[160,16,512]{2,0,1:T(8,128)(2,1)S(1)} all-to-all(bf16[160,16,512]{2,0,1:T(8,128)(2,1)S(1)} %bitcast.13), channel_id=1, replica_groups=mesh['row'=4,'col'=2,'depth'=4] {'row','depth'}, dimensions={1} | all-to-all | bytes 5242880 | tf_op jit(solution)/shard_map/all_to_all | solution.py:31
  166.3 17.8 %all-gather.9.cloned.1.call-done = bf16[2560,2048]{1,0:T(8,128)(2,1)} async-done(((bf16[160,2048]{1,0:T(8,128)(2,1)}), bf16[2560,2048]{1,0:T(8,128)(2,1)}) %all-gather.9.cloned.1.call-update) | async-done | bytes 10485776 | tf_op jit(solution)/shard_map/all_gather | solution.py:36
  184.1 0.0 copy-start
  184.1 18.9 %fusion = (bf16[512,2048]{1,0:T(8,128)(2,1)}, f32[512,2048]{1,0:T(8,128)}, f32[512,2048]{1,0:T(8,128)}, f32[512,2048]{1,0:T(8,128)}) fusion(f32[512,2048]{1,0:T(8,128)} %param.9, f32[512,2048]{1,0:T(8,128)} %param.10, f32[512,2048]{1,0:T(8,128)} %param.11, bf16[2560,512]{1,0:T(8,128)(2,1)S(1)} %bitcast.15, bf16[2560,2048]{1,0:T(8,128)(2,1)} %all-gather.9.cloned.1.call-done), kind=kOutput, calls=%fused_computation.5 | convolution fusion | flops 5386534912 | bytes 40370176 | tf_op jit(solution)/shard_map/dot_general | solution.py:34
  203.0 0.0 all-gather.11.cloned.1.call-update
  203.0 0.0 reduce-scatter.2.cloned.1.call-start
  203.1 542.1 %all-gather.7.cloned.1.call-done = bf16[8192,2048]{1,0:T(8,128)(2,1)} async-done(((bf16[2048,2048]{1,0:T(8,128)(2,1)}), bf16[8192,2048]{1,0:T(8,128)(2,1)}) %all-gather.7.cloned.1.call-update) | async-done | bytes 33554448 | tf_op jit(solution)/shard_map/all_gather | solution.py:21
  745.2 0.0 copy-done
  745.2 19.8 %fusion.1 = f32[160,8192]{1,0:T(8,128)} fusion(bf16[160,2048]{1,0:T(8,128)(2,1)S(1)} %copy-done, bf16[8192,2048]{1,0:T(8,128)(2,1)} %all-gather.7.cloned.1.call-done), kind=kOutput, calls=%fused_computation.6 | convolution fusion | flops 5368709120 | bytes 39452672 | tf_op jit(solution)/shard_map/dot_general | solution.py:25
  765.0 0.0 copy-start.1
  765.0 0.0 reduce-scatter.2.cloned.1.call-update
  765.1 38.1 %all-gather.11.cloned.1.call-done = bf16[2048,2048]{1,0:T(8,128)(2,1)} async-done(((bf16[512,2048]{1,0:T(8,128)(2,1)}), bf16[2048,2048]{1,0:T(8,128)(2,1)}) %all-gather.11.cloned.1.call-update) | async-done | bytes 8388624 | tf_op jit(solution)/shard_map/all_gather | solution.py:46
  803.1 0.0 copy-done.1
  803.1 15.2 %convolution_convert_fusion = bf16[160,2048]{1,0:T(8,128)(2,1)} fusion(bf16[160,8192]{1,0:T(8,128)(2,1)S(1)} %copy-done.1, bf16[8192,2048]{1,0:T(8,128)(2,1)} %all-gather.7.cloned.1.call-done), kind=kOutput, calls=%fused_computation.4 | convolution fusion | flops 5369036800 | bytes 36831232 | tf_op jit(solution)/shard_map/dot_general | solution.py:22
  818.3 53.3 %reduce-scatter.2.cloned.1.call-done = f32[160,4096]{1,0:T(8,128)} async-done(((f32[160,8192]{1,0:T(8,128)}), f32[160,4096]{1,0:T(8,128)}) %reduce-scatter.2.cloned.1.call-update) | async-done | bytes 2621456 | tf_op jit(solution)/shard_map/reduce_scatter | solution.py:28
  871.6 3.0 convert_element_type.10
  874.6 8.4 copy.18
Async XLA Ops:
  7.2 44.1 %all-gather.5.cloned.1.call-start = ((), (), s32[]{:S(2)}) async-start(), calls=%async_computation.2 | async-start | bytes 3932160 | tf_op jit(solution)/shard_map/all_gather | solution.py:20
  7.9 176.2 %all-gather.9.cloned.1.call-start = ((), (), s32[]{:S(2)}) async-start(), calls=%async_computation.5 | async-start | bytes 11141120 | tf_op jit(solution)/shard_map/all_gather | solution.py:36
  8.6 736.6 %all-gather.7.cloned.1.call-start = ((), (), s32[]{:S(2)}) async-start(), calls=%async_computation.3 | async-start | bytes 41943040 | tf_op jit(solution)/shard_map/all_gather | solution.py:21
  9.4 793.7 %all-gather.11.cloned.1.call-start = ((), (), s32[]{:S(2)}) async-start(), calls=%async_computation.6 | async-start | bytes 10485760 | tf_op jit(solution)/shard_map/all_gather | solution.py:46
  184.1 561.1 %copy-start = (bf16[160,2048]{1,0:T(8,128)(2,1)S(1)}, bf16[160,2048]{1,0:T(8,128)(2,1)}, u32[]{:S(2)}) copy-start(bf16[160,2048]{1,0:T(8,128)(2,1)} %param.8) | copy-start | bytes 1966084
  203.0 668.6 %reduce-scatter.2.cloned.1.call-start = ((), (), s32[]{:S(2)}) async-start(), calls=%async_computation.4 | async-start | bytes 7864320 | tf_op jit(solution)/shard_map/reduce_scatter | solution.py:28
  765.0 38.1 %copy-start.1 = (bf16[160,8192]{1,0:T(8,128)(2,1)S(1)}, bf16[160,8192]{1,0:T(8,128)(2,1)}, u32[]{:S(2)}) copy-start(bf16[160,8192]{1,0:T(8,128)(2,1)} %all-gather.5.cloned.1.call-done) | copy-start | bytes 7864324
Sparse Core Ops, SparseCore 0:
  9.5 41.7 all-gather.4
  53.6 130.5 all-gather.8
  185.7 559.5 all-gather.6
  746.6 56.4 all-gather.10
  805.8 65.7 reduce-scatter.1
where the time goes:
time: 890 us
  waiting for transfers between devices  695 us (78%)
  blocking collectives  113 us (13%)
  matrix products  53.9 us (6%)
  between operations  13.8 us (2%)
  local copies, waits for them, and re-layouts  10.4 us (1%)
    all_gather x1, waiting for transfers between devices, local(): full_panel = lax.all_gather(weight, 'row', axis=0, tiled=True)  542 us
    all_to_all x1, blocking collectives, local(): lax.all_to_all(full_rows, ('row', 'depth'), split_axis=1, concat_axis=0,...  113 us
    reduce_scatter x1, waiting for transfers between devices, local(): lax.psum_scatter(partial_value, 'col', scatter_dimension=1, tiled=True)  53.3 us
    all_gather x1, waiting for transfers between devices, local(): full_rows = lax.all_gather(tokens, 'col', axis=1, tiled=True)  41.8 us
    all_gather x1, waiting for transfers between devices, local(): new_weight = lax.all_gather(shard_weight, 'depth', axis=0, tiled=True)  38.1 us
    dot_general x1, matrix products, local(): lax.dot_general(cotangent, full_panel, (((1,), (1,)), ((), ())), preferre...  19.8 us
    dot_general x1, matrix products, local(): lax.dot_general(token_slab, lax.all_gather(cotangent, ('row', 'depth'), a...  18.9 us
    all_gather x1, waiting for transfers between devices, local(): lax.all_gather(cotangent, ('row', 'depth'), axis=0, tiled=True)  17.8 us
  transfers between devices with their start and end apart: 5, of which 5 were waited for; matrix products, arithmetic and copies ran while one was open for 6% of the time, Pallas kernels for 0%

commit v1 on v0

--- a/solution.py
+++ b/solution.py
@@ -15,25 +15,35 @@
 
 
 def local(tokens, weight, cotangent, master, first_moment, second_moment):
-    total_tokens = tokens.shape[0] * lax.axis_size("row") * lax.axis_size("depth")
+    rows, cols = lax.axis_size("row"), lax.axis_size("col")
+    block = tokens.shape[0]
+    total_tokens = block * rows * lax.axis_size("depth")
     grad_scale = 1.0 / math.sqrt(total_tokens)
     full_rows = lax.all_gather(tokens, "col", axis=1, tiled=True)
-    full_panel = lax.all_gather(weight, "row", axis=0, tiled=True)
-    queries = jnp.dot(full_rows, full_panel, preferred_element_type=jnp.float32).astype(
+    line_cotangent = lax.all_gather(cotangent, "row", axis=0, tiled=True)
+    line_tokens = lax.all_to_all(full_rows, "row", split_axis=1, concat_axis=0, tiled=True)
+    partial_grad = lax.dot_general(
+        line_cotangent, weight, (((1,), (1,)), ((), ())), preferred_element_type=jnp.float32
+    )
+    piece = lax.psum_scatter(partial_grad, "col", scatter_dimension=1, tiled=True).astype(
         jnp.bfloat16
     )
-    partial_value = lax.dot_general(
-        cotangent, full_panel, (((1,), (1,)), ((), ())), preferred_element_type=jnp.float32
-    )
-    token_grad = lax.psum_scatter(partial_value, "col", scatter_dimension=1, tiled=True).astype(
+    partial_queries = jnp.dot(line_tokens, weight, preferred_element_type=jnp.float32)
+    queries = lax.psum_scatter(partial_queries, "row", scatter_dimension=0, tiled=True).astype(
         jnp.bfloat16
     )
-    token_slab = lax.all_to_all(
-        full_rows, ("row", "depth"), split_axis=1, concat_axis=0, tiled=True
+    piece = lax.all_to_all(
+        piece.reshape(rows, block, -1), "row", split_axis=0, concat_axis=0, tiled=True
     )
+    piece = lax.all_to_all(
+        piece.reshape(cols, rows // cols, block, -1), "col", split_axis=0, concat_axis=0, tiled=True
+    )
+    token_grad = piece.transpose(2, 1, 0, 3).reshape(tokens.shape)
+    token_slab = lax.all_to_all(line_tokens, "depth", split_axis=1, concat_axis=0, tiled=True)
+    all_cotangent = lax.all_gather(line_cotangent, "depth", axis=0, tiled=True)
     product = lax.dot_general(
         token_slab,
-        lax.all_gather(cotangent, ("row", "depth"), axis=0, tiled=True),
+        all_cotangent,
         (((0,), (0,)), ((), ())),
         preferred_element_type=jnp.float32,
     )

time: 890 us -> 442 us (0.50)
  waiting for transfers between devices: 695 us -> 181 us
  blocking collectives: 113 us -> 181 us
  matrix products: 53.9 us -> 39 us
  local copies, waits for them, and re-layouts: 10.4 us -> 22.1 us
    all_gather x2, waiting for transfers between devices: 560 us -> 58.4 us  [the longest x1 58.3 us: local(): line_cotangent = lax.all_gather(cotangent, 'row', axis=0, tiled=True)]
    all_to_all x1 -> x4, blocking collectives: 113 us -> 181 us  [the longest x1 70.7 us: local(): lax.all_to_all(piece.reshape(rows, block, -1), 'row', split_axis=0, conca...]
    all_gather x1, waiting for transfers between devices: 38.1 us -> 62.7 us  [local(): new_weight = lax.all_gather(shard_weight, 'depth', axis=0, tiled=True)]
    reduce_scatter x1 -> x2, waiting for transfers between devices: 53.3 us -> 30.1 us  [the longest x1 24.3 us: local(): lax.psum_scatter(partial_queries, 'row', scatter_dimension=0, tiled=True)]
    dot_general x3, matrix products: 53.9 us -> 39 us  [the longest x1 18.4 us: local(): lax.dot_general(token_slab, all_cotangent, (((0,), (0,)), ((), ())), pref...]
    all_gather x1, waiting for transfers between devices: 41.8 us -> 28.1 us  [local(): full_rows = lax.all_gather(tokens, 'col', axis=1, tiled=True)]
  transfers between devices with their start and end apart: 5 -> 6, of which waited for: 5 -> 5; matrix products, arithmetic and copies ran while one was open for 6% -> 12% of each run, Pallas kernels for 0% -> 0%
where the time goes in v1:
time: 442 us
  waiting for transfers between devices  181 us (41%)
  blocking collectives  181 us (41%)
  matrix products  39 us (9%)
  local copies, waits for them, and re-layouts  22.1 us (5%)
  between operations  14.1 us (3%)
    all_to_all x1, blocking collectives, local(): lax.all_to_all(piece.reshape(rows, block, -1), 'row', split_axis=0, conca...  70.7 us
    all_to_all x1, blocking collectives, local(): lax.all_to_all(full_rows, 'row', split_axis=1, concat_axis=0, tiled=True)  63.7 us
    all_gather x1, waiting for transfers between devices, local(): new_weight = lax.all_gather(shard_weight, 'depth', axis=0, tiled=True)  62.7 us
    all_gather x1, waiting for transfers between devices, local(): line_cotangent = lax.all_gather(cotangent, 'row', axis=0, tiled=True)  58.3 us
    all_to_all x1, blocking collectives, local(): lax.all_to_all(line_tokens, 'depth', split_axis=1, concat_axis=0, tiled=T...  33.8 us
    all_gather x1, waiting for transfers between devices, local(): full_rows = lax.all_gather(tokens, 'col', axis=1, tiled=True)  28.1 us
    reduce_scatter x1, waiting for transfers between devices, local(): lax.psum_scatter(partial_queries, 'row', scatter_dimension=0, tiled=True)  24.3 us
    dot_general x1, matrix products, local(): lax.dot_general(token_slab, all_cotangent, (((0,), (0,)), ((), ())), pref...  18.4 us
  transfers between devices with their start and end apart: 6, of which 5 were waited for; matrix products, arithmetic and copies ran while one was open for 12% of the time, Pallas kernels for 0%

profile of v1, /device:TPU:0, one launch (start us, length us, event | category | flops | bytes accessed | tf_op | source)
XLA Modules:
  0.0 441.7 jit_solution(11255023881615150435)
XLA Ops:
  7.2 0.0 all-gather.7.cloned.1.call-start
  7.2 0.7 all-gather.7.cloned.1.call-update
  7.9 0.0 all-gather.5.cloned.1.call-start
  7.9 0.7 all-gather.5.cloned.1.call-update
  8.6 0.0 all-gather.9.cloned.1.call-start
  8.7 58.3 %all-gather.7.cloned.1.call-done = bf16[640,2048]{1,0:T(8,128)(2,1)} async-done(((bf16[160,2048]{1,0:T(8,128)(2,1)}), bf16[640,2048]{1,0:T(8,128)(2,1)}) %all-gather.7.cloned.1.call-update) | async-done | bytes 2621456 | tf_op jit(solution)/shard_map/all_gather | solution.py:23
  67.0 0.0 all-gather.9.cloned.1.call-update
  67.1 0.0 reduce-scatter.5.cloned.1.call-start
  67.1 11.1 %fusion.2 = f32[640,2048]{1,0:T(8,128)} fusion(bf16[640,2048]{1,0:T(8,128)(2,1)} %all-gather.7.cloned.1.call-done, bf16[2048,2048]{1,0:T(8,128)(2,1)} %param.7), kind=kOutput, calls=%fused_computation.6 | convolution fusion | flops 5368709120 | bytes 16252928 | tf_op jit(solution)/shard_map/dot_general | solution.py:25
  78.2 0.0 reduce-scatter.5.cloned.1.call-update
  78.2 0.0 reduce-scatter.3.cloned.1.call-start
  78.3 28.1 %all-gather.5.cloned.1.call-done = bf16[160,8192]{1,0:T(8,128)(2,1)} async-done(((bf16[160,4096]{1,0:T(8,128)(2,1)}), bf16[160,8192]{1,0:T(8,128)(2,1)}) %all-gather.5.cloned.1.call-update) | async-done | bytes 2621456 | tf_op jit(solution)/shard_map/all_gather | solution.py:22
  106.4 2.1 copy.27
  108.4 63.7 %all_to_all.48 = bf16[160,4,2048]{2,0,1:T(8,128)(2,1)S(1)} all-to-all(bf16[160,4,2048]{2,0,1:T(8,128)(2,1)S(1)} %bitcast.21), channel_id=1, replica_groups=mesh['row'=4,'col'=2,'depth'=4] {'row'}, dimensions={1} | all-to-all | bytes 5242880 | tf_op jit(solution)/shard_map/all_to_all | solution.py:24
  172.1 9.4 %fusion.1 = f32[640,2048]{1,0:T(8,128)} fusion(bf16[640,2048]{1,0:T(8,128)(2,1)S(1)} %bitcast.19, bf16[2048,2048]{1,0:T(8,128)(2,1)} %param.7), kind=kOutput, calls=%fused_computation.5 | convolution fusion | flops 5368709120 | bytes 16252928 | tf_op jit(solution)/shard_map/dot_general | solution.py:31
  181.6 0.0 all-gather.11.cloned.1.call-start
  181.6 3.5 all_to_all.40
  185.2 2.9 copy.24
  188.1 33.8 %all_to_all.49 = bf16[640,4,512]{2,0,1:T(8,128)(2,1)S(1)} all-to-all(bf16[640,4,512]{2,0,1:T(8,128)(2,1)S(1)} %copy.24), channel_id=1, replica_groups=mesh['row'=4,'col'=2,'depth'=4] {'depth'}, dimensions={1} | all-to-all | bytes 5242880 | tf_op jit(solution)/shard_map/all_to_all | solution.py:42
  221.9 18.4 %fusion = (bf16[512,2048]{1,0:T(8,128)(2,1)}, f32[512,2048]{1,0:T(8,128)}, f32[512,2048]{1,0:T(8,128)}, f32[512,2048]{1,0:T(8,128)}) fusion(f32[512,2048]{1,0:T(8,128)} %param.9, f32[512,2048]{1,0:T(8,128)} %param.10, f32[512,2048]{1,0:T(8,128)} %param.11, bf16[2560,512]{1,0:T(8,128)(2,1)S(1)} %bitcast.26, bf16[2560,2048]{1,0:T(8,128)(2,1)} %all-gather.9.cloned.1.call-done), kind=kOutput, calls=%fused_computation.4 | convolution fusion | flops 5386534912 | bytes 40370176 | tf_op jit(solution)/shard_map/dot_general | solution.py:44
  240.3 0.0 all-gather.11.cloned.1.call-update
  240.3 5.8 %reduce-scatter.5.cloned.1.call-done = f32[640,1024]{1,0:T(8,128)} async-done(((f32[640,2048]{1,0:T(8,128)}), f32[640,1024]{1,0:T(8,128)}) %reduce-scatter.5.cloned.1.call-update) | async-done | bytes 2621456 | tf_op jit(solution)/shard_map/reduce_scatter | solution.py:28
  246.1 1.9 convert_element_type.10
  248.0 70.7 %all_to_all.50 = bf16[4,160,1024]{2,1,0:T(8,128)(2,1)S(1)} all-to-all(bf16[4,160,1024]{2,1,0:T(8,128)(2,1)S(1)} %bitcast.24), channel_id=1, replica_groups=mesh['row'=4,'col'=2,'depth'=4] {'row'}, dimensions={0} | all-to-all | bytes 2621440 | tf_op jit(solution)/shard_map/all_to_all | solution.py:35
  318.7 1.3 copy.22
  320.1 13.3 %all_to_all.51 = bf16[2,2,160,1024]{3,1,2,0:T(2,128)(2,1)S(1)} all-to-all(bf16[2,2,160,1024]{3,1,2,0:T(2,128)(2,1)S(1)} %copy.22), channel_id=1, replica_groups=mesh['row'=4,'col'=2,'depth'=4] {'col'}, dimensions={0} | all-to-all | bytes 2621440 | tf_op jit(solution)/shard_map/all_to_all | solution.py:38
  333.3 2.0 copy.23
  335.4 1.8 reshape.30
  337.2 24.3 %reduce-scatter.3.cloned.1.call-done = f32[160,2048]{1,0:T(8,128)} async-done(((f32[640,2048]{1,0:T(8,128)}), f32[160,2048]{1,0:T(8,128)}) %reduce-scatter.3.cloned.1.call-update) | async-done | bytes 1310736 | tf_op jit(solution)/shard_map/reduce_scatter | solution.py:32
  361.5 2.2 convert_element_type.9
  363.8 62.7 %all-gather.11.cloned.1.call-done = bf16[2048,2048]{1,0:T(8,128)(2,1)} async-done(((bf16[512,2048]{1,0:T(8,128)(2,1)}), bf16[2048,2048]{1,0:T(8,128)(2,1)}) %all-gather.11.cloned.1.call-update) | async-done | bytes 8388624 | tf_op jit(solution)/shard_map/all_gather | solution.py:56
  426.4 8.4 %copy.29 = bf16[2048,2048]{1,0:T(8,128)(2,1)} copy(bf16[2048,2048]{1,0:T(8,128)(2,1)} %all-gather.11.cloned.1.call-done) | data formatting | bytes 16777216
  (2 shorter events, 0.0 us)
Async XLA Ops:
  7.2 59.9 %all-gather.7.cloned.1.call-start = ((), (), s32[]{:S(2)}) async-start(), calls=%async_computation.8 | async-start | bytes 3276800 | tf_op jit(solution)/shard_map/all_gather | solution.py:23
  7.9 98.5 %all-gather.5.cloned.1.call-start = ((), (), s32[]{:S(2)}) async-start(), calls=%async_computation.6 | async-start | bytes 3932160 | tf_op jit(solution)/shard_map/all_gather | solution.py:22
  8.6 213.2 %all-gather.9.cloned.1.call-start = ((), (), s32[]{:S(2)}) async-start(), calls=%async_computation.10 | async-start | bytes 13107200 | tf_op jit(solution)/shard_map/all_gather | solution.py:43
  67.1 179.0 %reduce-scatter.5.cloned.1.call-start = ((), (), s32[]{:S(2)}) async-start(), calls=%async_computation.9 | async-start | bytes 7864320 | tf_op jit(solution)/shard_map/reduce_scatter | solution.py:28
  78.2 283.3 %reduce-scatter.3.cloned.1.call-start = ((), (), s32[]{:S(2)}) async-start(), calls=%async_computation.7 | async-start | bytes 6553600 | tf_op jit(solution)/shard_map/reduce_scatter | solution.py:32
  181.6 244.9 %all-gather.11.cloned.1.call-start = ((), (), s32[]{:S(2)}) async-start(), calls=%async_computation.11 | async-start | bytes 10485760 | tf_op jit(solution)/shard_map/all_gather | solution.py:56
Sparse Core Ops, SparseCore 0:
  9.5 57.4 all-gather.6
  68.6 37.7 all-gather.4
  107.9 70.1 all-gather.8
  180.3 65.7 reduce-scatter.4
  248.8 112.6 reduce-scatter.2
  362.9 63.4 all-gather.10
